TPU v7x, 32 devices: a whole 2x2x4 slice. The times are simulated.
32 devices in a mesh: dp: 8 (over y, x, core), seq: 4 (over z).
Axes of the slice: x: 2, y: 2, z: 4, core: 2. Of those that a mesh axis runs over, the one named last changes fastest.
Arguments:
- states: bfloat16 [4096, 1280], P(('dp', 'seq')), parts along dimension 0, may hold values from -90 to 90
- token_kind: int32 [4096], P(('dp', 'seq')), parts along dimension 0, may hold values from 0 to 3
- episode: int32 [4096], P(('dp', 'seq')), parts along dimension 0, may hold values from 0 to 3, never falling along the last dimension, each value on 1 to 384 neighbouring positions
- kind_table: bfloat16 [4, 1280], replicated, may hold values from -3 to 3
- w_qkv: bfloat16 [1280, 3072], replicated, may hold values from -0.15625 to 0.15625
- w_out: bfloat16 [1024, 1280], replicated, may hold values from -0.1875 to 0.1875
Outputs:
- attended: bfloat16 [4096, 1280], P(('dp', 'seq')), parts along dimension 0
There are 8 independent parts, one for each index of `dp`. A program takes and returns all parts, laid end to end along the dimension named above; an argument that names none is the same for every part. Nothing has to cross between parts.
All inputs are finite; a program needn't handle non-finite values.
Results may differ from a plain program's by a relative error of at most 0.0055.
The roundings to bfloat16 on the way count: a program that leaves them out, or rounds other values in their place, can miss the bound.
Values may be sent and summed in bfloat16 or wider, within the bound.
No kernel may reach another device: no remote copies, remote signals or barrier semaphores. Data moves between devices by JAX's collectives and lax.ppermute only.
A program may use at most 128 MiB of HBM per device.

v0:
```python
import math
import jax
import jax.numpy as jnp
from jax import lax
from jax.sharding import PartitionSpec as P

HEADS = 16


def absorb(
    running, queries, query_place, query_episode, key_rows, value_rows, key_place, key_episode
):
    maxima, totals, summed = running
    temper = 1.0 / math.sqrt(queries.shape[2])
    scores = (
        jnp.einsum("qhd,khd->hqk", queries, key_rows, preferred_element_type=jnp.float32) * temper
    )
    allowed = (key_place[None, :] <= query_place[:, None]) & (
        key_episode[None, :] == query_episode[:, None]
    )
    scores = jnp.where(allowed[None], scores, -1e30)
    raised = jnp.maximum(maxima, jnp.max(scores, axis=2))
    shrink = jnp.exp(maxima - raised)
    weights = jnp.where(allowed[None], jnp.exp(scores - raised[:, :, None]), 0.0)
    totals = totals * shrink + jnp.sum(weights, axis=2)
    summed = summed * shrink.T[:, :, None] + jnp.einsum(
        "hqk,khd->qhd", weights.astype(jnp.bfloat16), value_rows, preferred_element_type=jnp.float32
    )
    return (raised, totals, summed)


def sweep_keys(
    running, queries, query_place, query_episode, key_rows, value_rows, key_place, key_episode
):
    length = key_rows.shape[0]
    stride = math.gcd(length, 512)

    def visit(number, current):
        offset = number * stride
        keys_here = lax.dynamic_slice_in_dim(key_rows, offset, stride, 0)
        values_here = lax.dynamic_slice_in_dim(value_rows, offset, stride, 0)
        place_here = lax.dynamic_slice_in_dim(key_place, offset, stride, 0)
        episode_here = lax.dynamic_slice_in_dim(key_episode, offset, stride, 0)
        skipped = (place_here[0] > query_place[-1]) | (episode_here[-1] < query_episode[0])
        return lax.cond(
            skipped,
            lambda s: s,
            lambda s: absorb(
                s,
                queries,
                query_place,
                query_episode,
                keys_here,
                values_here,
                place_here,
                episode_here,
            ),
            current,
        )

    return lax.fori_loop(0, length // stride, visit, running)


def fresh_state(count, heads, head_size):
    return (
        jnp.full((heads, count), -1e30, jnp.float32),
        jnp.zeros((heads, count), jnp.float32),
        jnp.zeros((count, heads, head_size), jnp.float32),
    )


def local(states, token_kind, episode, kind_table, w_qkv, w_out):
    rows = states.shape[0]
    kinds = kind_table.shape[0]
    picked = (token_kind[:, None] == jnp.arange(kinds, dtype=jnp.int32)[None, :]).astype(
        jnp.float32
    )
    added = jnp.dot(picked, kind_table.astype(jnp.float32), precision=lax.Precision.HIGHEST)
    inputs = (states.astype(jnp.float32) + added).astype(jnp.bfloat16)
    projected = jnp.dot(inputs, w_qkv, preferred_element_type=jnp.float32).astype(jnp.bfloat16)
    inner = w_out.shape[0]
    head_size = inner // HEADS
    queries = projected[:, :inner].reshape(rows, HEADS, head_size)
    key_flat = projected[:, inner : 2 * inner]
    value_flat = projected[:, 2 * inner :]
    key_three = key_flat.reshape(rows, HEADS, head_size)
    value_three = value_flat.reshape(rows, HEADS, head_size)
    moved_q, moved_k, moved_v = (
        lax.all_to_all(queries, "seq", split_axis=1, concat_axis=0, tiled=True),
        lax.all_to_all(key_three, "seq", split_axis=1, concat_axis=0, tiled=True),
        lax.all_to_all(value_three, "seq", split_axis=1, concat_axis=0, tiled=True),
    )
    whole_episode = lax.all_gather(episode, "seq", axis=0, tiled=True)
    length = moved_q.shape[0]
    local_heads = moved_q.shape[1]
    whole_place = jnp.arange(length, dtype=jnp.int32)
    stride = math.gcd(length, 512)

    def query_block(number, written):
        offset = number * stride
        block_q = lax.dynamic_slice_in_dim(moved_q, offset, stride, 0)
        block_place = lax.dynamic_slice_in_dim(whole_place, offset, stride, 0)
        block_episode = lax.dynamic_slice_in_dim(whole_episode, offset, stride, 0)
        maxima, totals, summed = sweep_keys(
            fresh_state(stride, local_heads, head_size),
            block_q,
            block_place,
            block_episode,
            moved_k,
            moved_v,
            whole_place,
            whole_episode,
        )
        result = (summed / totals.T[:, :, None]).astype(jnp.bfloat16)
        return lax.dynamic_update_slice_in_dim(written, result, offset, 0)

    written = lax.fori_loop(
        0, length // stride, query_block, jnp.zeros((length, local_heads, head_size), jnp.bfloat16)
    )
    heads_out = lax.all_to_all(written, "seq", split_axis=0, concat_axis=1, tiled=True).reshape(
        rows, inner
    )
    return jnp.dot(heads_out, w_out, preferred_element_type=jnp.float32).astype(jnp.bfloat16)


def solution(mesh):
    placed = (P(("dp", "seq"), None), P(("dp", "seq")), P(("dp", "seq")), P(), P(), P())
    return jax.shard_map(
        local, mesh=mesh, in_specs=placed, out_specs=P(("dp", "seq"), None), check_vma=False
    )
```

profile of v0, /device:TPU:0, one launch (start us, length us, event | category | flops | bytes accessed | tf_op | source)
XLA Modules:
  0.0 70.3 jit_solution(8716372642339516466)
XLA Ops:
  0.0 0.0 copy-start
  0.0 1.4 %fusion.23 = bf16[128,1280]{1,0:T(8,128)(2,1)S(1)} fusion(bf16[4,1280]{1,0:T(4,128)(2,1)} %param.11, bf16[128,1280]{1,0:T(8,128)(2,1)} %param.8, s32[128]{0:T(128)} %param.9), kind=kOutput, calls=%fused_computation.26 | convolution fusion | flops 1802752 | bytes 666112 | tf_op jit(solution)/shard_map/dot_general | solution.py:78
  1.4 4.5 %convolution_convert_fusion = bf16[128,3072]{1,0:T(8,128)(2,1)S(1)} fusion(bf16[128,1280]{1,0:T(8,128)(2,1)S(1)} %fusion.23, bf16[1280,3072]{1,0:T(8,128)(2,1)} %param.12), kind=kOutput, calls=%fused_computation.24 | convolution fusion | flops 1007026176 | bytes 8978432 | tf_op jit(solution)/shard_map/dot_general | solution.py:80
  6.0 0.0 copy-start.2
  6.0 0.1 fusion.25
  6.1 0.8 %copy.37 = bf16[128,1024]{0,1:T(8,128)(2,1)} copy(bf16[128,1024]{1,0:T(8,128)(2,1)S(1)} %get-tuple-element.182) | data formatting | bytes 524288 | tf_op jit(solution)/shard_map/slice | solution.py:85
  6.9 6.3 %all-to-all-start.2 = ((bf16[128,16,64]{0,2,1:T(8,128)(2,1)}), bf16[128,16,64]{0,2,1:T(8,128)(2,1)S(1)}, u32[]{:S(2)}, u32[]{:S(2)}) async-start(bf16[128,16,64]{0,2,1:T(8,128)(2,1)} %bitcast.11), calls=%async_computation.2 | async-start | bytes 524288 | tf_op jit(solution)/shard_map/all_to_all | solution.py:91
  13.2 0.8 %copy.36 = bf16[128,1024]{0,1:T(8,128)(2,1)} copy(bf16[128,1024]{1,0:T(8,128)(2,1)S(1)} %get-tuple-element.183) | data formatting | bytes 524288 | tf_op jit(solution)/shard_map/slice | solution.py:84
  14.1 8.1 %all-to-all-done.2 = bf16[128,16,64]{0,2,1:T(8,128)(2,1)S(1)} async-done(((bf16[128,16,64]{0,2,1:T(8,128)(2,1)}), bf16[128,16,64]{0,2,1:T(8,128)(2,1)S(1)}, u32[]{:S(2)}, u32[]{:S(2)}) %all-to-all-start.2) | async-done | bytes 262176 | tf_op jit(solution)/shard_map/all_to_all | solution.py:91
  22.2 3.4 %all-to-all-start.1 = ((bf16[128,16,64]{0,2,1:T(8,128)(2,1)}), bf16[128,16,64]{0,2,1:T(8,128)(2,1)S(1)}, u32[]{:S(2)}, u32[]{:S(2)}) async-start(bf16[128,16,64]{0,2,1:T(8,128)(2,1)} %bitcast.8), calls=%async_computation.1 | async-start | bytes 524288 | tf_op jit(solution)/shard_map/all_to_all | solution.py:90
  25.6 0.8 %copy.35 = bf16[128,1024]{0,1:T(8,128)(2,1)} copy(bf16[128,1024]{1,0:T(8,128)(2,1)S(1)} %get-tuple-element.184) | data formatting | bytes 524288 | tf_op jit(solution)/shard_map/slice | solution.py:83
  26.4 6.2 %all-to-all-done.1 = bf16[128,16,64]{0,2,1:T(8,128)(2,1)S(1)} async-done(((bf16[128,16,64]{0,2,1:T(8,128)(2,1)}), bf16[128,16,64]{0,2,1:T(8,128)(2,1)S(1)}, u32[]{:S(2)}, u32[]{:S(2)}) %all-to-all-start.1) | async-done | bytes 262176 | tf_op jit(solution)/shard_map/all_to_all | solution.py:90
  32.6 0.0 copy-start.1
  32.6 4.0 %all-to-all-start = ((bf16[128,16,64]{0,2,1:T(8,128)(2,1)}), bf16[128,16,64]{0,2,1:T(8,128)(2,1)}, u32[]{:S(2)}, u32[]{:S(2)}) async-start(bf16[128,16,64]{0,2,1:T(8,128)(2,1)} %bitcast.5), calls=%async_computation | async-start | bytes 524288 | tf_op jit(solution)/shard_map/all_to_all | solution.py:89
  36.6 0.0 copy-done.2
  36.6 11.3 %all-gather = s32[4,1,128]{2,1,0:T(1,128)S(1)} all-gather(s32[1,1,128]{2,1,0:T(1,128)S(1)} %bitcast.64), channel_id=1, replica_groups=mesh['dp'=8,'seq'=4] {'seq'}, dimensions={0}, use_global_device_ids=true | all-gather | bytes 2560 | tf_op jit(solution)/shard_map/all_gather | solution.py:93
  47.9 0.6 fusion.26
  49.8 0.6 fusion.27
  51.7 0.0 copy-done.1
  51.7 0.1 broadcast.75
  51.8 0.0 all-to-all-done
  51.8 4.7 %conditional.1 = ((f32[4,512]{1,0:T(4,128)S(1)}, f32[512,4,64]{0,2,1:T(8,128)S(1)})) conditional(s32[]{:T(128)} %bitcast.4, (s32[512]{0:T(512)S(1)}, s32[512]{0:T(512)S(1)}, bf16[4,128,4,64]{1,3,2,0:T(8,128)(2,1)}, bf16[4,128,4,64]{1,3,2,0:T(8,128)(2,1)}, f32[4,512]{1,0:T(4,128)S(1)}, /*index=5*/f32[512,4,64]{0,2,1:T(8,128)S(1)}, ...), branch_computations={%region_0.3_spmd, %region_3.4_spmd} | conditional | flops 283121664 | bytes 15568920 | solution.py:45
  51.8 0.3 compare_and_fusion
  52.1 1.9 %fusion = (f32[4,512]{1,0:T(4,128)S(1)}, f32[4,512,512]{1,2,0:T(8,128)S(1)}) fusion(pred[512,512]{0,1:T(8,128)(4,1)S(1)} %compare_and_fusion, bf16[4,128,4,64]{1,3,2,0:T(8,128)(2,1)} %get-tuple-element.174, bf16[4,128,4,64]{1,3,2,0:T(8,128)(2,1)} %get-tuple-element.173), kind=kOutput, calls=%fused_computation.2 | convolution fusion | flops 137361408 | bytes 4988928 | tf_op jit(solution)/shard_map/while/body/eval_jaxpr/while/body/eval_jaxpr/cond/branch_0_fun/qhd,khd->hqk/dot_general | solution.py:16
  54.0 1.0 %fusion.2 = f32[4,512]{1,0:T(4,128)S(1)} fusion(f32[4,512,512]{1,2,0:T(8,128)S(1)} %get-tuple-element.181, f32[4,512]{1,0:T(4,128)S(1)} %broadcast_maximum_fusion, pred[512,512]{0,1:T(8,128)(4,1)S(1)} %compare_and_fusion), kind=kLoop, calls=%fused_computation.4 | loop fusion | flops 5240832 | bytes 4472832 | tf_op jit(solution)/shard_map/while/body/eval_jaxpr/while/body/eval_jaxpr/cond/branch_0_fun/reduce_sum | solution.py:25
  55.1 1.4 %fusion.9 = f32[512,4,64]{0,2,1:T(8,128)S(1)} fusion(f32[4,512,512]{1,2,0:T(8,128)S(1)} %get-tuple-element.181, f32[4,512]{1,0:T(4,128)S(1)} %broadcast_maximum_fusion, pred[512,512]{0,1:T(8,128)(4,1)S(1)} %compare_and_fusion, f32[512,4,64]{0,2,1:T(8,128)S(1)} %get-tuple-element.144, f32[512,4]{0,1:T(4,128)S(1)} %get-tuple-element.178, ...), kind=kOutput, calls=%fused_computation.8 | convolution fusion | flops 139722752 | bytes 5783552 | tf_op jit(solution)/shard_map/while/body/eval_jaxpr/while/body/eval_jaxpr/cond/branch_0_fun/hqk,khd->qhd/dot_general | solution.py:26
  56.5 0.1 divide_convert_fusion
  56.5 0.3 copy.41
  56.9 0.4 reshape.84
  57.3 10.2 %all_to_all.72 = bf16[4,2,16384]{2,1,0:T(2,128)(2,1)} all-to-all(bf16[4,2,16384]{2,1,0:T(2,128)(2,1)S(1)} %reshape.84), channel_id=1, replica_groups=mesh['dp'=8,'seq'=4] {'seq'}, dimensions={0} | all-to-all | bytes 524288 | tf_op jit(solution)/shard_map/all_to_all | solution.py:120
  67.4 1.3 %reshape.85 = bf16[512,4,64]{2,1,0:T(4,128)(2,1)S(1)} reshape(bf16[4,2,16384]{2,1,0:T(2,128)(2,1)} %all_to_all.72) | data formatting | bytes 524288
  68.8 0.3 copy.43
  69.0 0.0 copy-done
  69.1 1.3 %convolution_convert_fusion.1 = bf16[128,1280]{1,0:T(8,128)(2,1)} fusion(bf16[128,1024]{0,1:T(8,128)(2,1)S(1)} %bitcast.58, bf16[1024,1280]{1,0:T(8,128)(2,1)S(1)} %copy-done), kind=kOutput, calls=%fused_computation.27 | convolution fusion | flops 335708160 | bytes 3211264 | tf_op jit(solution)/shard_map/dot_general | solution.py:123
  (5 shorter events, 0.0 us)
Async XLA Ops:
  0.0 69.0 %copy-start = (bf16[1024,1280]{1,0:T(8,128)(2,1)S(1)}, bf16[1024,1280]{1,0:T(8,128)(2,1)}, u32[]{:S(2)}) copy-start(bf16[1024,1280]{1,0:T(8,128)(2,1)} %param.13) | copy-start | bytes 7864324
  6.0 30.6 %copy-start.2 = (s32[128]{0:T(128)S(1)}, s32[128]{0:T(128)}, u32[]{:S(2)}) copy-start(s32[128]{0:T(128)} %param.10) | copy-start | bytes 1540
  6.9 15.3 %all-to-all-start.2 = ((bf16[128,16,64]{0,2,1:T(8,128)(2,1)}), bf16[128,16,64]{0,2,1:T(8,128)(2,1)S(1)}, u32[]{:S(2)}, u32[]{:S(2)}) async-start(bf16[128,16,64]{0,2,1:T(8,128)(2,1)} %bitcast.11), calls=%async_computation.2 | async-start | bytes 524288 | tf_op jit(solution)/shard_map/all_to_all | solution.py:91
  22.2 10.4 %all-to-all-start.1 = ((bf16[128,16,64]{0,2,1:T(8,128)(2,1)}), bf16[128,16,64]{0,2,1:T(8,128)(2,1)S(1)}, u32[]{:S(2)}, u32[]{:S(2)}) async-start(bf16[128,16,64]{0,2,1:T(8,128)(2,1)} %bitcast.8), calls=%async_computation.1 | async-start | bytes 524288 | tf_op jit(solution)/shard_map/all_to_all | solution.py:90
  32.6 19.1 %copy-start.1 = (bf16[128,16,64]{0,2,1:T(8,128)(2,1)}, bf16[128,16,64]{0,2,1:T(8,128)(2,1)S(1)}, u32[]{:S(2)}) copy-start(bf16[128,16,64]{0,2,1:T(8,128)(2,1)S(1)} %all-to-all-done.1) | copy-start | bytes 786436
  32.6 19.2 %all-to-all-start = ((bf16[128,16,64]{0,2,1:T(8,128)(2,1)}), bf16[128,16,64]{0,2,1:T(8,128)(2,1)}, u32[]{:S(2)}, u32[]{:S(2)}) async-start(bf16[128,16,64]{0,2,1:T(8,128)(2,1)} %bitcast.5), calls=%async_computation | async-start | bytes 524288 | tf_op jit(solution)/shard_map/all_to_all | solution.py:89
where the time goes:
time: 70.9 us; the launch traced here: 70.3 us
  blocking collectives  21.5 us (30%)
  waiting for transfers between devices  14.2 us (20%)
  starting transfers between devices  13.8 us (19%)
  matrix products  10.5 us (15%)
  local copies, waits for them, and re-layouts  6.16 us (9%)
  between operations  2.67 us (4%)
  other arithmetic  1.4 us (2%)
    all_gather x1, blocking collectives, local(): whole_episode = lax.all_gather(episode, 'seq', axis=0, tiled=True)  11.3 us
    all_to_all x1, blocking collectives, local(): lax.all_to_all(written, 'seq', split_axis=0, concat_axis=1, tiled=True)  10.2 us
    all_to_all x1, waiting for transfers between devices, local(): lax.all_to_all(value_three, 'seq', split_axis=1, concat_axis=0, tiled=True)  8.07 us
    all_to_all x1, starting transfers between devices, local(): lax.all_to_all(value_three, 'seq', split_axis=1, concat_axis=0, tiled=True)  6.35 us
    all_to_all x1, waiting for transfers between devices, local(): lax.all_to_all(key_three, 'seq', split_axis=1, concat_axis=0, tiled=True)  6.16 us
    dot_general x1, matrix products, local(): jnp.dot(inputs, w_qkv, preferred_element_type=jnp.float32)  4.53 us
    all_to_all x1, starting transfers between devices, local(): lax.all_to_all(queries, 'seq', split_axis=1, concat_axis=0, tiled=True)  4.04 us
    all_to_all x1, starting transfers between devices, local(): lax.all_to_all(key_three, 'seq', split_axis=1, concat_axis=0, tiled=True)  3.4 us
  transfers between devices with their start and end apart: 3, of which 2 were waited for; matrix products, arithmetic and copies ran while one was open for 4% of the time, Pallas kernels for 0%

commit v1 on v0

--- a/solution.py
+++ b/solution.py
@@ -117,9 +117,15 @@
     written = lax.fori_loop(
         0, length // stride, query_block, jnp.zeros((length, local_heads, head_size), jnp.bfloat16)
     )
-    heads_out = lax.all_to_all(written, "seq", split_axis=0, concat_axis=1, tiled=True).reshape(
-        rows, inner
-    )
+    heads_out = jnp.concatenate(
+        lax.all_to_all(
+            jnp.stack(jnp.split(written, lax.axis_size("seq"), 0)),
+            axis_name="seq",
+            split_axis=0,
+            concat_axis=0,
+        ),
+        axis=1,
+    ).reshape(rows, inner)
     return jnp.dot(heads_out, w_out, preferred_element_type=jnp.float32).astype(jnp.bfloat16)
 
 

time: 70.9 us -> 68.1 us (0.961)
  local copies, waits for them, and re-layouts: 6.16 us -> 3.95 us
    unnamed x8 -> x6, local copies, waits for them, and re-layouts: 1.74 us -> 0.01 us
where the time goes in v1:
time: 68.1 us; the launch traced here: 67.6 us
  blocking collectives  20.8 us (31%)
  waiting for transfers between devices  14.2 us (21%)
  starting transfers between devices  13.8 us (20%)
  matrix products  10.5 us (15%)
  local copies, waits for them, and re-layouts  3.95 us (6%)
  between operations  2.74 us (4%)
  other arithmetic  1.43 us (2%)
    all_gather x1, blocking collectives, local(): whole_episode = lax.all_gather(episode, 'seq', axis=0, tiled=True)  11.3 us
    all_to_all x1, blocking collectives, local(): lax.all_to_all(jnp.stack(jnp.split(written, lax.axis_size('seq'), 0)), ax...  9.51 us
    all_to_all x1, waiting for transfers between devices, local(): lax.all_to_all(value_three, 'seq', split_axis=1, concat_axis=0, tiled=True)  8.07 us
    all_to_all x1, starting transfers between devices, local(): lax.all_to_all(value_three, 'seq', split_axis=1, concat_axis=0, tiled=True)  6.35 us
    all_to_all x1, waiting for transfers between devices, local(): lax.all_to_all(key_three, 'seq', split_axis=1, concat_axis=0, tiled=True)  6.16 us
    dot_general x1, matrix products, local(): jnp.dot(inputs, w_qkv, preferred_element_type=jnp.float32)  4.53 us
    all_to_all x1, starting transfers between devices, local(): lax.all_to_all(queries, 'seq', split_axis=1, concat_axis=0, tiled=True)  4.05 us
    all_to_all x1, starting transfers between devices, local(): lax.all_to_all(key_three, 'seq', split_axis=1, concat_axis=0, tiled=True)  3.4 us
  transfers between devices with their start and end apart: 3, of which 2 were waited for; matrix products, arithmetic and copies ran while one was open for 4% of the time, Pallas kernels for 0%

profile of v1, /device:TPU:0, one launch (start us, length us, event | category | flops | bytes accessed | tf_op | source)
XLA Modules:
  0.0 67.6 jit_solution(10843802326198403439)
XLA Ops:
  0.0 0.0 copy-start
  0.0 1.4 %fusion.23 = bf16[128,1280]{1,0:T(8,128)(2,1)S(1)} fusion(bf16[4,1280]{1,0:T(4,128)(2,1)} %param.11, bf16[128,1280]{1,0:T(8,128)(2,1)} %param.8, s32[128]{0:T(128)} %param.9), kind=kOutput, calls=%fused_computation.26 | convolution fusion | flops 1802752 | bytes 666112 | tf_op jit(solution)/shard_map/dot_general | solution.py:78
  1.4 4.5 %convolution_convert_fusion = bf16[128,3072]{1,0:T(8,128)(2,1)S(1)} fusion(bf16[128,1280]{1,0:T(8,128)(2,1)S(1)} %fusion.23, bf16[1280,3072]{1,0:T(8,128)(2,1)} %param.12), kind=kOutput, calls=%fused_computation.24 | convolution fusion | flops 1007026176 | bytes 8978432 | tf_op jit(solution)/shard_map/dot_general | solution.py:80
  6.0 0.0 copy-start.2
  6.0 0.1 fusion.25
  6.1 0.8 %copy.18 = bf16[128,1024]{0,1:T(8,128)(2,1)} copy(bf16[128,1024]{1,0:T(8,128)(2,1)S(1)} %get-tuple-element.168) | data formatting | bytes 524288 | tf_op jit(solution)/shard_map/slice | solution.py:85
  6.9 6.3 %all-to-all-start.2 = ((bf16[128,16,64]{0,2,1:T(8,128)(2,1)}), bf16[128,16,64]{0,2,1:T(8,128)(2,1)S(1)}, u32[]{:S(2)}, u32[]{:S(2)}) async-start(bf16[128,16,64]{0,2,1:T(8,128)(2,1)} %bitcast.11), calls=%async_computation.2 | async-start | bytes 524288 | tf_op jit(solution)/shard_map/all_to_all | solution.py:91
  13.2 0.8 %copy.17 = bf16[128,1024]{0,1:T(8,128)(2,1)} copy(bf16[128,1024]{1,0:T(8,128)(2,1)S(1)} %get-tuple-element.169) | data formatting | bytes 524288 | tf_op jit(solution)/shard_map/slice | solution.py:84
  14.1 8.1 %all-to-all-done.2 = bf16[128,16,64]{0,2,1:T(8,128)(2,1)S(1)} async-done(((bf16[128,16,64]{0,2,1:T(8,128)(2,1)}), bf16[128,16,64]{0,2,1:T(8,128)(2,1)S(1)}, u32[]{:S(2)}, u32[]{:S(2)}) %all-to-all-start.2) | async-done | bytes 262176 | tf_op jit(solution)/shard_map/all_to_all | solution.py:91
  22.2 3.4 %all-to-all-start.1 = ((bf16[128,16,64]{0,2,1:T(8,128)(2,1)}), bf16[128,16,64]{0,2,1:T(8,128)(2,1)S(1)}, u32[]{:S(2)}, u32[]{:S(2)}) async-start(bf16[128,16,64]{0,2,1:T(8,128)(2,1)} %bitcast.8), calls=%async_computation.1 | async-start | bytes 524288 | tf_op jit(solution)/shard_map/all_to_all | solution.py:90
  25.6 0.8 %copy.16 = bf16[128,1024]{0,1:T(8,128)(2,1)} copy(bf16[128,1024]{1,0:T(8,128)(2,1)S(1)} %get-tuple-element.170) | data formatting | bytes 524288 | tf_op jit(solution)/shard_map/slice | solution.py:83
  26.4 6.2 %all-to-all-done.1 = bf16[128,16,64]{0,2,1:T(8,128)(2,1)S(1)} async-done(((bf16[128,16,64]{0,2,1:T(8,128)(2,1)}), bf16[128,16,64]{0,2,1:T(8,128)(2,1)S(1)}, u32[]{:S(2)}, u32[]{:S(2)}) %all-to-all-start.1) | async-done | bytes 262176 | tf_op jit(solution)/shard_map/all_to_all | solution.py:90
  32.6 0.0 copy-start.1
  32.6 4.1 %all-to-all-start = ((bf16[128,16,64]{0,2,1:T(8,128)(2,1)}), bf16[128,16,64]{0,2,1:T(8,128)(2,1)}, u32[]{:S(2)}, u32[]{:S(2)}) async-start(bf16[128,16,64]{0,2,1:T(8,128)(2,1)} %bitcast.5), calls=%async_computation | async-start | bytes 524288 | tf_op jit(solution)/shard_map/all_to_all | solution.py:89
  36.6 0.0 copy-done.2
  36.6 11.3 %all-gather = s32[4,1,128]{2,1,0:T(1,128)S(1)} all-gather(s32[1,1,128]{2,1,0:T(1,128)S(1)} %bitcast.69), channel_id=1, replica_groups=mesh['dp'=8,'seq'=4] {'seq'}, dimensions={0}, use_global_device_ids=true | all-gather | bytes 2560 | tf_op jit(solution)/shard_map/all_gather | solution.py:93
  48.0 0.6 fusion.26
  49.9 0.6 fusion.27
  51.8 0.0 copy-done.1
  51.8 0.1 broadcast.75
  51.9 0.0 all-to-all-done
  51.9 4.7 %conditional.1 = ((f32[4,512]{1,0:T(4,128)S(1)}, f32[512,4,64]{0,2,1:T(8,128)S(1)})) conditional(s32[]{:T(128)} %bitcast.4, (s32[512]{0:T(512)S(1)}, s32[512]{0:T(512)S(1)}, bf16[4,128,4,64]{1,3,2,0:T(8,128)(2,1)}, bf16[4,128,4,64]{1,3,2,0:T(8,128)(2,1)}, f32[4,512]{1,0:T(4,128)S(1)}, /*index=5*/f32[512,4,64]{0,2,1:T(8,128)S(1)}, ...), branch_computations={%region_0.3_spmd, %region_3.4_spmd} | conditional | flops 283121664 | bytes 15568920 | solution.py:45
  51.9 0.3 compare_and_fusion
  52.2 1.9 %fusion = (f32[4,512]{1,0:T(4,128)S(1)}, f32[4,512,512]{1,2,0:T(8,128)S(1)}) fusion(pred[512,512]{0,1:T(8,128)(4,1)S(1)} %compare_and_fusion, bf16[4,128,4,64]{1,3,2,0:T(8,128)(2,1)} %get-tuple-element.160, bf16[4,128,4,64]{1,3,2,0:T(8,128)(2,1)} %get-tuple-element.159), kind=kOutput, calls=%fused_computation.2 | convolution fusion | flops 137361408 | bytes 4988928 | tf_op jit(solution)/shard_map/while/body/eval_jaxpr/while/body/eval_jaxpr/cond/branch_0_fun/qhd,khd->hqk/dot_general | solution.py:16
  54.2 1.0 %fusion.2 = f32[4,512]{1,0:T(4,128)S(1)} fusion(f32[4,512,512]{1,2,0:T(8,128)S(1)} %get-tuple-element.167, f32[4,512]{1,0:T(4,128)S(1)} %broadcast_maximum_fusion, pred[512,512]{0,1:T(8,128)(4,1)S(1)} %compare_and_fusion), kind=kLoop, calls=%fused_computation.4 | loop fusion | flops 5240832 | bytes 4472832 | tf_op jit(solution)/shard_map/while/body/eval_jaxpr/while/body/eval_jaxpr/cond/branch_0_fun/reduce_sum | solution.py:25
  55.2 1.4 %fusion.9 = f32[512,4,64]{0,2,1:T(8,128)S(1)} fusion(f32[4,512,512]{1,2,0:T(8,128)S(1)} %get-tuple-element.167, f32[4,512]{1,0:T(4,128)S(1)} %broadcast_maximum_fusion, pred[512,512]{0,1:T(8,128)(4,1)S(1)} %compare_and_fusion, f32[512,4,64]{0,2,1:T(8,128)S(1)} %get-tuple-element.144, f32[512,4]{0,1:T(4,128)S(1)} %get-tuple-element.164, ...), kind=kOutput, calls=%fused_computation.8 | convolution fusion | flops 139722752 | bytes 5783552 | tf_op jit(solution)/shard_map/while/body/eval_jaxpr/while/body/eval_jaxpr/cond/branch_0_fun/hqk,khd->qhd/dot_general | solution.py:26
  56.6 0.1 divide_convert_fusion
  56.7 0.1 slice_bitcast_fusion.3
  56.8 9.5 %all_to_all.62 = bf16[4,128,4,64]{1,3,2,0:T(8,128)(2,1)S(1)} all-to-all(bf16[4,128,4,64]{1,3,2,0:T(8,128)(2,1)S(1)} %pad_maximum_fusion), channel_id=1, replica_groups=mesh['dp'=8,'seq'=4] {'seq'}, dimensions={0} | all-to-all | bytes 524288 | tf_op jit(solution)/shard_map/all_to_all | solution.py:121
  66.3 0.0 copy-done
  66.3 1.3 %convolution_convert_fusion.1 = bf16[128,1280]{1,0:T(8,128)(2,1)} fusion(bf16[128,1024]{0,1:T(8,128)(2,1)S(1)} %bitcast.63, bf16[1024,1280]{1,0:T(8,128)(2,1)S(1)} %copy-done), kind=kOutput, calls=%fused_computation.27 | convolution fusion | flops 335708160 | bytes 3211264 | tf_op jit(solution)/shard_map/dot_general | solution.py:129
  (6 shorter events, 0.1 us)
Async XLA Ops:
  0.0 66.3 %copy-start = (bf16[1024,1280]{1,0:T(8,128)(2,1)S(1)}, bf16[1024,1280]{1,0:T(8,128)(2,1)}, u32[]{:S(2)}) copy-start(bf16[1024,1280]{1,0:T(8,128)(2,1)} %param.13) | copy-start | bytes 7864324
  6.0 30.7 %copy-start.2 = (s32[128]{0:T(128)S(1)}, s32[128]{0:T(128)}, u32[]{:S(2)}) copy-start(s32[128]{0:T(128)} %param.10) | copy-start | bytes 1540
  6.9 15.3 %all-to-all-start.2 = ((bf16[128,16,64]{0,2,1:T(8,128)(2,1)}), bf16[128,16,64]{0,2,1:T(8,128)(2,1)S(1)}, u32[]{:S(2)}, u32[]{:S(2)}) async-start(bf16[128,16,64]{0,2,1:T(8,128)(2,1)} %bitcast.11), calls=%async_computation.2 | async-start | bytes 524288 | tf_op jit(solution)/shard_map/all_to_all | solution.py:91
  22.2 10.4 %all-to-all-start.1 = ((bf16[128,16,64]{0,2,1:T(8,128)(2,1)}), bf16[128,16,64]{0,2,1:T(8,128)(2,1)S(1)}, u32[]{:S(2)}, u32[]{:S(2)}) async-start(bf16[128,16,64]{0,2,1:T(8,128)(2,1)} %bitcast.8), calls=%async_computation.1 | async-start | bytes 524288 | tf_op jit(solution)/shard_map/all_to_all | solution.py:90
  32.6 19.2 %copy-start.1 = (bf16[128,16,64]{0,2,1:T(8,128)(2,1)}, bf16[128,16,64]{0,2,1:T(8,128)(2,1)S(1)}, u32[]{:S(2)}) copy-start(bf16[128,16,64]{0,2,1:T(8,128)(2,1)S(1)} %all-to-all-done.1) | copy-start | bytes 786436
  32.6 19.3 %all-to-all-start = ((bf16[128,16,64]{0,2,1:T(8,128)(2,1)}), bf16[128,16,64]{0,2,1:T(8,128)(2,1)}, u32[]{:S(2)}, u32[]{:S(2)}) async-start(bf16[128,16,64]{0,2,1:T(8,128)(2,1)} %bitcast.5), calls=%async_computation | async-start | bytes 524288 | tf_op jit(solution)/shard_map/all_to_all | solution.py:89
